TPU v7x, 32 devices: a whole 2x2x4 slice. The times are simulated.
32 devices in a mesh: seq: 8 (over y, x, core), req: 4 (over z).
Axes of the slice: x: 2, y: 2, z: 4, core: 2. Of those that a mesh axis runs over, the one named last changes fastest.
Arguments:
- queries: bfloat16 [8, 256, 1536], P('req', 'seq'), as said below
- new_kv: bfloat16 [2, 8, 256, 512], P(None, 'req', 'seq'), may hold values from -6 to 6
- cache_kv: bfloat16 [2, 8, 2048, 512], P(None, 'req', 'seq'), as said below
- cache_spans: int32 [8, 2], P('req'), may hold values from 0 to 2048, as said below
- recompute_rows: int32 [8, 256], P('req'), may hold values from 0 to 2047, as said below
- held_states: bfloat16 [8, 256, 1536], P('req', 'seq'), may hold values from -6 to 6
- key_weight: bfloat16 [1536, 512], replicated, may hold values from -0.15625 to 0.15625
- norm_gain: float32 [1536], replicated, may hold values from 0.1 to 1.9
- routes: int32 [8, 256, 8], P('req', 'seq'), may hold values from 0 to 19, all different within a row; in each aligned block of 32 rows (0 to 31, 32 to 63, ..., all dimensions but the last counted through in order) at most 16 rows name the same one
- route_weights: float32 [8, 256, 8], P('req', 'seq'), may hold values from 0.05 to 1
- expert_gate_up: bfloat16 [20, 1536, 1024], P('req'), may hold values from -0.15625 to 0.15625
- expert_down: bfloat16 [20, 512, 1536], P('req'), may hold values from -0.25 to 0.25
Outputs:
- layer_out: bfloat16 [8, 256, 1536], P('req', 'seq')
Inputs may be any that keep to these rules, and one draw needn't show every extreme that they name: `routes`: in each aligned block of 32 rows of one request (one device's rows of that request) no expert is named more than 16 times. cache_spans[r] = (start, length): 1024 <= length <= 2048 with some request of length 2048; 0 <= start <= 512 with some request starting at 0. `recompute_rows`: within a request the rows are distinct and lie between the request's start and length. `queries`: entries lie within -6 to 6. `cache_kv`: entries lie within -6 to 6.
All inputs are finite; a program needn't handle non-finite values.
Results may differ from a plain program's by a relative error of at most 0.034.
Values may be sent and summed in bfloat16 or wider, within the bound.
A program may use at most 192 MiB of HBM per device.

v0:
```python
import jax
import jax.numpy as jnp
from jax import lax
from jax.sharding import PartitionSpec as P

H = 24
KVH = 8
HD = 64
FF = 512
TOP = 8
CAP = 16
NEG = -1e30
THETA = 10000.0


def rotate(key_heads, positions):
    half_dim = key_heads.shape[-1] // 2
    exponent = jnp.arange(half_dim).astype(jnp.float32) * (2.0 / key_heads.shape[-1])
    inverse = THETA ** (-exponent)
    angles = positions.astype(jnp.float32)[..., None] * inverse
    cosine = jnp.cos(angles)[..., None, :]
    sine_part = jnp.sin(angles)[..., None, :]
    lower_half = key_heads[..., :half_dim]
    upper_half = key_heads[..., half_dim:]
    return jnp.concatenate(
        [
            lower_half * cosine - upper_half * sine_part,
            upper_half * cosine + lower_half * sine_part,
        ],
        axis=-1,
    )


def partial_attend(packed):
    query_rows, key_rows, value_rows, allowed = packed
    query_count, model_width = query_rows.shape
    key_count = key_rows.shape[0]
    groups = H // KVH
    query_heads = query_rows.reshape(query_count, KVH, groups, HD)
    key_heads = key_rows.reshape(key_count, KVH, HD)
    value_heads = value_rows.reshape(key_count, KVH, HD)
    scores = jnp.einsum(
        "qkgd,nkd->kgqn", query_heads, key_heads, preferred_element_type=jnp.float32
    ) * HD ** (-0.5)
    scores = jnp.where(allowed[None, None, :, :], scores, NEG)
    highest = jnp.max(scores, axis=-1, keepdims=True)
    exps = jnp.exp(scores - highest)
    totals = jnp.sum(exps, axis=-1)
    weights = exps.astype(jnp.bfloat16)
    mixed_rows = jnp.einsum(
        "kgqn,nkd->qkgd", weights, value_heads, preferred_element_type=jnp.float32
    )
    mixed_rows = mixed_rows / jnp.transpose(totals, (2, 0, 1))[..., None]
    log_total = highest[..., 0] + jnp.log(totals)
    log_rows = jnp.transpose(log_total, (2, 0, 1)).reshape(query_count, H)
    return (mixed_rows.reshape(query_count, model_width), log_rows)


def body(
    queries,
    new_kv,
    cache_kv,
    cache_spans,
    recompute_rows,
    held_states,
    key_weight,
    norm_gain,
    routes,
    route_weights,
    expert_gate_up,
    expert_down,
):
    seq_index = lax.axis_index("seq")
    seq_count = lax.axis_size("seq")
    owner_count = lax.axis_size("req")
    req_rows, tok_rows, model_width = queries.shape
    cache_rows = cache_kv.shape[2]
    held_rows = held_states.shape[1]
    local_experts = expert_gate_up.shape[0]
    expert_total = owner_count * local_experts
    my_positions = lax.dynamic_slice_in_dim(recompute_rows, seq_index * held_rows, held_rows, 1)
    projected = jnp.dot(
        held_states.reshape(req_rows * held_rows, model_width),
        key_weight,
        preferred_element_type=jnp.float32,
    )
    rotated = rotate(projected.reshape(req_rows, held_rows, KVH, HD), my_positions)
    rotated = rotated.reshape(req_rows, held_rows, KVH * HD).astype(jnp.bfloat16)
    fresh_rows = lax.all_gather(rotated, "seq", axis=1, tiled=True)
    cache_positions = seq_index * cache_rows + jnp.arange(cache_rows)
    hit_table = recompute_rows[:, None, :] == cache_positions[None, :, None]
    placed = jnp.einsum(
        "rcm,rmk->rck",
        hit_table.astype(jnp.bfloat16),
        fresh_rows,
        preferred_element_type=jnp.float32,
    ).astype(jnp.bfloat16)
    cache_keys = jnp.where(jnp.any(hit_table, axis=2)[:, :, None], placed, cache_kv[0])
    span_start = cache_spans[:, 0:1]
    span_end = cache_spans[:, 1:2]
    all_queries = lax.all_gather(queries, "seq", axis=1, tiled=True)
    step_total = all_queries.shape[1]
    cache_allowed = (cache_positions[None, :] >= span_start) & (cache_positions[None, :] < span_end)
    key_positions = seq_index * tok_rows + jnp.arange(tok_rows)
    step_allowed = key_positions[None, :] <= jnp.arange(step_total)[:, None]
    allowed = jnp.concatenate(
        [
            jnp.broadcast_to(cache_allowed[:, None, :], (req_rows, step_total, cache_rows)),
            jnp.broadcast_to(step_allowed[None], (req_rows, step_total, tok_rows)),
        ],
        axis=2,
    )
    key_rows = jnp.concatenate([cache_keys, new_kv[0]], axis=1)
    value_rows = jnp.concatenate([cache_kv[1], new_kv[1]], axis=1)
    part_out, part_log = lax.map(partial_attend, (all_queries, key_rows, value_rows, allowed))
    piece_out, piece_log = (
        lax.all_to_all(part_out[None], "seq", split_axis=2, concat_axis=0, tiled=True),
        lax.all_to_all(part_log[None], "seq", split_axis=2, concat_axis=0, tiled=True),
    )
    best_log = jnp.max(piece_log, axis=0)
    factors = jnp.exp(piece_log - best_log[None])
    factor_sum = jnp.sum(factors, axis=0)
    spread_out = piece_out.reshape(seq_count, req_rows, tok_rows, H, HD)
    combined = jnp.sum(spread_out * factors[..., None], axis=0) / factor_sum[..., None]
    attended_f = combined.reshape(req_rows, tok_rows, model_width)
    attended = attended_f.astype(jnp.bfloat16)
    attended_f = attended.astype(jnp.float32)
    mean_square = jnp.mean(attended_f * attended_f, axis=-1, keepdims=True)
    normed = (attended_f * lax.rsqrt(mean_square + 1e-06) * norm_gain).astype(jnp.bfloat16)
    route_flat = routes.reshape(req_rows, tok_rows * TOP)
    expert_match = (route_flat[:, :, None] == jnp.arange(expert_total)[None, None, :]).astype(
        jnp.int32
    )
    earlier = jnp.cumsum(expert_match, axis=1) - expert_match
    slot_index = jnp.sum(earlier * expert_match, axis=2)
    target = route_flat * CAP + slot_index
    slot_match = target[:, :, None] == jnp.arange(expert_total * CAP)[None, None, :]
    dispatch = jnp.any(
        slot_match.reshape(req_rows, tok_rows, TOP, expert_total * CAP), axis=2
    ).astype(jnp.bfloat16)
    dispatch = dispatch.reshape(req_rows, tok_rows, owner_count, local_experts, CAP)
    outgoing = jnp.einsum(
        "rtnec,rtd->nrecd", dispatch, normed, preferred_element_type=jnp.float32
    ).astype(jnp.bfloat16)
    hidden = jnp.einsum(
        "srecd,edf->srecf",
        lax.all_to_all(outgoing, "req", split_axis=0, concat_axis=0, tiled=True),
        expert_gate_up,
        preferred_element_type=jnp.float32,
    )
    active = (jax.nn.silu(hidden[..., :FF]) * hidden[..., FF:]).astype(jnp.bfloat16)
    result = jnp.einsum(
        "srecf,efd->srecd", active, expert_down, preferred_element_type=jnp.float32
    ).astype(jnp.bfloat16)
    returned = lax.all_to_all(result, "req", split_axis=0, concat_axis=0, tiled=True)
    owner_of = route_flat // local_experts
    local_of = route_flat % local_experts
    flat_index = (
        (owner_of * req_rows + jnp.arange(req_rows)[:, None]) * local_experts + local_of
    ) * CAP + slot_index
    returned_rows = jnp.take(returned.reshape(-1, model_width), flat_index.reshape(-1), axis=0)
    returned_rows = returned_rows.reshape(req_rows, tok_rows, TOP, model_width)
    mixture = jnp.einsum(
        "rtk,rtkd->rtd",
        route_weights,
        returned_rows.astype(jnp.float32),
        precision=lax.Precision.HIGHEST,
    )
    return (attended_f + mixture).astype(jnp.bfloat16)


def solution(mesh):
    in_specs = (
        P("req", "seq", None),
        P(None, "req", "seq", None),
        P(None, "req", "seq", None),
        P("req", None),
        P("req", None),
        P("req", "seq", None),
        P(),
        P(),
        P("req", "seq", None),
        P("req", "seq", None),
        P("req", None, None),
        P("req", None, None),
    )
    out_specs = P("req", "seq", None)
    return jax.shard_map(body, mesh=mesh, in_specs=in_specs, out_specs=out_specs, check_vma=False)
```

profile of v0, /device:TPU:2, one launch (start us, length us, event | category | flops | bytes accessed | tf_op | source)
XLA Modules:
  0.0 298.9 jit_solution(2745684699913608374)
XLA Ops:
  6.5 1.8 copy.65
  9.2 1.7 copy.63
  13.4 10.8 %all_gather.6 = bf16[2,256,512]{2,1,0:T(8,128)(2,1)S(1)} all-gather(bf16[2,32,512]{2,1,0:T(8,128)(2,1)S(1)} %convert_element_type.67), channel_id=1, replica_groups=mesh['seq'=8,'req'=4] {'seq'}, dimensions={1}, use_global_device_ids=true | all-gather | bytes 589824 | tf_op jit(solution)/shard_map/all_gather | solution.py:89
  27.1 10.3 %all-gather.2.cloned.1.call-done = bf16[2,256,1536]{2,0,1:T(2,128)(2,1)} async-done(((bf16[2,32,1536]{2,0,1:T(2,128)(2,1)}), bf16[2,256,1536]{2,0,1:T(2,128)(2,1)}) %all-gather.2.cloned.1.call-update) | async-done | bytes 1572880 | tf_op jit(solution)/shard_map/all_gather | solution.py:101
  37.4 4.9 %copy.67 = bf16[2,256,1536]{1,2,0:T(8,128)(2,1)} copy(bf16[2,256,1536]{2,0,1:T(2,128)(2,1)} %all-gather.2.cloned.1.call-done) | data formatting | bytes 3145728 | tf_op jit(solution)/shard_map/while | solution.py:115
  42.3 78.1 %while.12 = (s32[]{:T(128)}, f32[2,256,1536]{2,0,1:T(2,128)}, f32[2,256,24]{1,2,0:T(8,128)S(1)}, bf16[2,288,512]{1,2,0:T(8,128)(2,1)}, pred[2,256,288]{1,2,0:T(8...) while((s32[]{:T(128)}, f32[2,256,1536]{2,0,1:T(2,128)}, ...), condition=%wide.region_4.5_spmd, body=%wide.region_1.4_spmd.sunk | while | flops 472836096 | bytes 62791824 | solution.py:115
  49.9 4.8 %bitcast_divide_fusion.2 = f32[256,8,3,64]{0,3,2,1:T(8,128)S(1)} fusion(bf16[288,8,64,1]{0,2,3,1:T(8,128)(2,1)S(1)} %bitcast.165, f32[8,288,256,3]{2,1,3,0:T(8,128)} %copy-done.2, f32[8,3,256]{2,1,0:T(4,128)S(1)} %get-tuple-element.152, pred[256,288]{0,1:T(8,128)(4,1)S(1)} %dynamic-slice_bitcast_fusion.2, f32[256,8,3]{0,2,1:T(4,128)S(1)} %bitcast.167), kind=kOutput, calls=%fused_computation.8.clone.1 | convolution fusion | flops 233963520 | bytes 9068544 | tf_op jit(solution)/shard_map/while/body/eval_jaxpr/kgqn,nkd->qkgd/dot_general | solution.py:50
  55.9 25.4 %dynamic_update_slice.12 = f32[2,256,1536]{2,0,1:T(2,128)} dynamic-update-slice(f32[2,256,1536]{2,0,1:T(2,128)} %get-tuple-element.163, f32[1,256,1536]{2,0,1:T(1,128)S(1)} %copy.114, s32[]{:T(128)} %get-tuple-element.162, s32[]{:T(128)} %constant.54.clone.1..sunk, s32[]{:T(128)} %constant.54.clone.1..sunk) | dynamic-update-slice | bytes 3145732 | tf_op jit(solution)/shard_map/while/body/jit(dynamic_update_index_in_dim)/dynamic_update_slice | solution.py:115
  88.9 4.8 %bitcast_divide_fusion.2 = f32[256,8,3,64]{0,3,2,1:T(8,128)S(1)} fusion(bf16[288,8,64,1]{0,2,3,1:T(8,128)(2,1)S(1)} %bitcast.165, f32[8,288,256,3]{2,1,3,0:T(8,128)} %copy-done.2, f32[8,3,256]{2,1,0:T(4,128)S(1)} %get-tuple-element.152, pred[256,288]{0,1:T(8,128)(4,1)S(1)} %dynamic-slice_bitcast_fusion.2, f32[256,8,3]{0,2,1:T(4,128)S(1)} %bitcast.167), kind=kOutput, calls=%fused_computation.8.clone.1 | convolution fusion | flops 233963520 | bytes 9068544 | tf_op jit(solution)/shard_map/while/body/eval_jaxpr/kgqn,nkd->qkgd/dot_general | solution.py:50
  94.9 25.4 %dynamic_update_slice.12 = f32[2,256,1536]{2,0,1:T(2,128)} dynamic-update-slice(f32[2,256,1536]{2,0,1:T(2,128)} %get-tuple-element.163, f32[1,256,1536]{2,0,1:T(1,128)S(1)} %copy.114, s32[]{:T(128)} %get-tuple-element.162, s32[]{:T(128)} %constant.54.clone.1..sunk, s32[]{:T(128)} %constant.54.clone.1..sunk) | dynamic-update-slice | bytes 3145732 | tf_op jit(solution)/shard_map/while/body/jit(dynamic_update_index_in_dim)/dynamic_update_slice | solution.py:115
  120.9 6.6 %all_to_all.43 = f32[8,1,1536]{2,1,0:T(1,128)S(1)} all-to-all(f32[8,1,1536]{2,1,0:T(1,128)S(1)} %reshape.329), channel_id=1, replica_groups=mesh['seq'=8,'req'=4] {'seq'}, dimensions={0} | all-to-all | bytes 98304 | tf_op jit(solution)/shard_map/all_to_all | solution.py:118
  127.5 5.2 %all-to-all-start = ((f32[1,2,256,1536]{3,1,0,2:T(2,128)}), f32[1,2,256,1536]{3,1,0,2:T(2,128)S(1)}, u32[]{:S(2)}, u32[]{:S(2)}) async-start(f32[1,2,256,1536]{3,1,0,2:T(2,128)} %bitcast.168), calls=%async_computation | async-start | bytes 6291456 | tf_op jit(solution)/shard_map/all_to_all | solution.py:117
  140.2 1.8 copy.72
  142.0 4.9 %mul.189 = f32[8,2,32,24,64]{4,3,2,0,1:T(8,128)} broadcast(f32[8,2,32,24]{3,2,0,1:T(8,128)} %copy.72), dimensions={0,1,2,3} | broadcast | bytes 3194880 | tf_op jit(solution)/shard_map/mul | solution.py:124
  146.9 6.2 %mul.190 = f32[8,1,2,32,1536]{4,3,0,2,1:T(8,128)} reshape(f32[8,2,32,24,64]{4,3,2,0,1:T(8,128)} %mul.189) | data formatting | bytes 6291456 | tf_op jit(solution)/shard_map/mul | solution.py:124
  154.3 2.1 div.54
  156.4 12.6 %all-to-all-done = f32[1,2,256,1536]{3,1,0,2:T(2,128)S(1)} async-done(((f32[1,2,256,1536]{3,1,0,2:T(2,128)}), f32[1,2,256,1536]{3,1,0,2:T(2,128)S(1)}, u32[]{:S(2)}, u32[]{:S(2)}) %all-to-all-start) | async-done | bytes 3145760 | tf_op jit(solution)/shard_map/all_to_all | solution.py:117
  173.0 50.3 %all_to_all.44 = bf16[4,2,5,16,1536]{4,3,1,2,0:T(8,128)(2,1)S(1)} all-to-all(bf16[4,2,5,16,1536]{4,3,1,2,0:T(8,128)(2,1)S(1)} %copy.83), channel_id=1, replica_groups=mesh['seq'=8,'req'=4] {'req'}, dimensions={0} | all-to-all | bytes 3932160 | tf_op jit(solution)/shard_map/all_to_all | solution.py:147
  223.3 8.1 %fusion.22 = f32[4,2,5,16,1024]{4,3,1,0,2:T(8,128)S(1)} fusion(bf16[5,1536,1024]{2,1,0:T(8,128)(2,1)} %param.24, bf16[4,2,5,16,1536]{4,3,1,2,0:T(8,128)(2,1)S(1)} %all_to_all.44), kind=kOutput, calls=%fused_computation.27 | convolution fusion | flops 2013265920 | bytes 20316160 | tf_op jit(solution)/shard_map/srecd,edf->srecf/dot_general | solution.py:145
  234.2 4.5 %all-to-all-start.3 = ((bf16[4,2,5,16,1536]{4,3,1,2,0:T(8,128)(2,1)}), bf16[4,2,5,16,1536]{4,3,1,2,0:T(8,128)(2,1)}, u32[]{:S(2)}, u32[]{:S(2)}) async-start(bf16[4,2,5,16,1536]{4,3,1,2,0:T(8,128)(2,1)} %copy.85), calls=%async_computation.3 | async-start | bytes 3932160 | tf_op jit(solution)/shard_map/all_to_all | solution.py:155
  239.3 44.5 %all-to-all-done.3 = bf16[4,2,5,16,1536]{4,3,1,2,0:T(8,128)(2,1)} async-done(((bf16[4,2,5,16,1536]{4,3,1,2,0:T(8,128)(2,1)}), bf16[4,2,5,16,1536]{4,3,1,2,0:T(8,128)(2,1)}, u32[]{:S(2)}, u32[]{:S(2)}) %all-to-all-start.3) | async-done | bytes 1966112 | tf_op jit(solution)/shard_map/all_to_all | solution.py:155
  283.8 1.7 copy.86
  285.5 3.0 gather_fusion
  288.4 2.9 fusion.27
  (134 shorter events, 40.6 us)
Async XLA Ops:
  6.5 4.6 %copy-start = (bf16[2,32,1536]{2,1,0:T(8,128)(2,1)S(1)}, bf16[2,32,1536]{2,1,0:T(8,128)(2,1)}, u32[]{:S(2)}) copy-start(bf16[2,32,1536]{2,1,0:T(8,128)(2,1)} %param.19) | copy-start | bytes 589828
  6.5 30.8 %all-gather.2.cloned.1.call-start = ((), (), s32[]{:S(2)}) async-start(), calls=%async_computation.4 | async-start | bytes 1769472 | tf_op jit(solution)/shard_map/all_gather | solution.py:101
  10.9 1.6 copy-start.6
  12.0 1.0 slice-start
  12.1 1.1 copy-start.14
  12.3 12.3 %copy-start.13 = (s32[2,256]{1,0:T(2,128)S(1)}, s32[2,256]{1,0:T(2,128)}, u32[]{:S(2)}) copy-start(s32[2,256]{1,0:T(2,128)} %param.18) | copy-start | bytes 6148
  12.4 12.5 %copy-start.4 = (bf16[2,2,256,512]{3,2,1,0:T(8,128)(2,1)S(1)}, bf16[2,2,256,512]{3,2,1,0:T(8,128)(2,1)}, u32[]{:S(2)}) copy-start(bf16[2,2,256,512]{3,2,1,0:T(8,128)(2,1)} %param.16) | copy-start | bytes 3145732
  45.9 2.9 copy-start.2
  84.9 2.9 copy-start.2
  127.5 5.2 %copy-start.11 = (s32[2,32,8]{1,2,0:T(8,128)S(1)}, s32[2,32,8]{1,2,0:T(8,128)}, u32[]{:S(2)}) copy-start(s32[2,32,8]{1,2,0:T(8,128)} %param.22) | copy-start | bytes 6148
  127.5 41.5 %all-to-all-start = ((f32[1,2,256,1536]{3,1,0,2:T(2,128)}), f32[1,2,256,1536]{3,1,0,2:T(2,128)S(1)}, u32[]{:S(2)}, u32[]{:S(2)}) async-start(f32[1,2,256,1536]{3,1,0,2:T(2,128)} %bitcast.168), calls=%async_computation | async-start | bytes 6291456 | tf_op jit(solution)/shard_map/all_to_all | solution.py:117
  134.6 0.7 copy-start.8
  146.9 6.2 %copy-start.7 = (f32[2,32,24]{1,2,0:T(8,128)S(1)}, f32[2,32,24]{1,2,0:T(8,128)}, u32[]{:S(2)}) copy-start(f32[2,32,24]{1,2,0:T(8,128)} %get-tuple-element.93) | copy-start | bytes 18436
  169.0 1.9 copy-start.3
  170.9 1.0 copy-start.5
  170.9 1.1 copy-start.10
  173.0 58.4 %slice-start.1 = ((s8[7864320]{0:T(1024)(128)(4,1)}), s8[4194304]{0:T(1024)(128)(4,1)S(1)}, s32[]{:S(2)}) async-start(s8[7864320]{0:T(1024)(128)(4,1)} %bitcast.179), calls=%async_computation.6 | async-start | bytes 8388608
  223.3 8.1 %slice-start.2 = ((s8[7864320]{0:T(1024)(128)(4,1)}), s8[3670016]{0:T(1024)(128)(4,1)S(1)}, s32[]{:S(2)}) async-start(s8[7864320]{0:T(1024)(128)(4,1)} %bitcast.179), calls=%async_computation.7 | async-start | bytes 7340032
  234.2 4.9 %copy-start.9 = (s32[2,256]{1,0:T(2,128)S(1)}, s32[2,256]{1,0:T(2,128)}, u32[]{:S(2)}) copy-start(s32[2,256]{1,0:T(2,128)} %copy-done.8) | copy-start | bytes 6148
  234.2 4.9 %copy-start.12 = (f32[2,32,8]{1,2,0:T(8,128)S(1)}, f32[2,32,8]{1,2,0:T(8,128)}, u32[]{:S(2)}) copy-start(f32[2,32,8]{1,2,0:T(8,128)} %param.23) | copy-start | bytes 6148
  234.2 49.5 %all-to-all-start.3 = ((bf16[4,2,5,16,1536]{4,3,1,2,0:T(8,128)(2,1)}), bf16[4,2,5,16,1536]{4,3,1,2,0:T(8,128)(2,1)}, u32[]{:S(2)}, u32[]{:S(2)}) async-start(bf16[4,2,5,16,1536]{4,3,1,2,0:T(8,128)(2,1)} %copy.85), calls=%async_computation.3 | async-start | bytes 3932160 | tf_op jit(solution)/shard_map/all_to_all | solution.py:155
  285.4 6.6 %copy-start.1 = (bf16[2,32,1536]{2,1,0:T(8,128)(2,1)S(1)}, bf16[2,32,1536]{2,1,0:T(8,128)(2,1)}, u32[]{:S(2)}) copy-start(bf16[2,32,1536]{2,1,0:T(8,128)(2,1)} %param.19) | copy-start | bytes 589828
Sparse Core Ops, SparseCore 0:
  9.2 28.0 all-gather.1
where the time goes:
time: 303 us; the launch traced here: 299 us
  local copies, waits for them, and re-layouts  102 us (34%)
  blocking collectives  67.7 us (22%)
  waiting for transfers between devices  67.4 us (22%)
  matrix products  26.3 us (9%)
  between operations  13.9 us (5%)
  other arithmetic  12 us (4%)
  starting transfers between devices  9.69 us (3%)
    dynamic_update_slice x6, local copies, waits for them, and re-layouts, body(): lax.map(partial_attend, (all_queries, key_rows, value_rows, allowed))  53.2 us
    all_to_all x1, blocking collectives, body(): lax.all_to_all(outgoing, 'req', split_axis=0, concat_axis=0, tiled=True)  50.3 us
    all_to_all x1, waiting for transfers between devices, body(): lax.all_to_all(result, 'req', split_axis=0, concat_axis=0, tiled=True)  44.5 us
    all_to_all x1, waiting for transfers between devices, body(): lax.all_to_all(part_out[None], 'seq', split_axis=2, concat_axis=0, tiled=...  12.6 us
    mul x2, local copies, waits for them, and re-layouts, body(): spread_out * factors[..., None]  11.1 us
    all_gather x1, blocking collectives, body(): fresh_rows = lax.all_gather(rotated, 'seq', axis=1, tiled=True)  10.8 us
    all_gather x1, waiting for transfers between devices, body(): all_queries = lax.all_gather(queries, 'seq', axis=1, tiled=True)  10.3 us
    dot_general x2, matrix products, partial_attend(): jnp.einsum('kgqn,nkd->qkgd', weights, value_heads, preferred_element_type...  9.64 us
  transfers between devices with their start and end apart: 3, of which 3 were waited for; matrix products, arithmetic and copies ran while one was open for 11% of the time, Pallas kernels for 0%

commit v1 on v0

--- a/solution.py
+++ b/solution.py
@@ -11,6 +11,18 @@
 CAP = 16
 NEG = -1e30
 THETA = 10000.0
+
+
+def cut_along(array, dim, peers):
+    dims = array.shape
+    blocks = array.reshape(*dims[:dim], peers, dims[dim] // peers, *dims[dim + 1 :])
+    return jnp.moveaxis(blocks, dim, 0)
+
+
+def joined_along(tiles, dim):
+    tiles = jnp.moveaxis(tiles, 0, dim)
+    shape = tiles.shape
+    return tiles.reshape(*shape[:dim], shape[dim] * shape[dim + 1], *shape[dim + 2 :])
 
 
 def rotate(key_heads, positions):
@@ -152,7 +164,14 @@
     result = jnp.einsum(
         "srecf,efd->srecd", active, expert_down, preferred_element_type=jnp.float32
     ).astype(jnp.bfloat16)
-    returned = lax.all_to_all(result, "req", split_axis=0, concat_axis=0, tiled=True)
+    size, index = (lax.axis_size("req"), lax.axis_index("req"))
+    parts = cut_along(result, 0, size)
+    finished = [parts[index]]
+    for lap in range(1, size):
+        sent = parts[index ^ lap]
+        finished.append(lax.ppermute(sent, "req", [(i, i ^ lap) for i in range(size)]))
+    parts = jnp.stack(finished)[index ^ jnp.arange(size)]
+    returned = joined_along(parts, 0)
     owner_of = route_flat // local_experts
     local_of = route_flat % local_experts
     flat_index = (

time: 303 us -> 304 us (level)
  the two profiles are of different devices: /device:TPU:2 before, /device:TPU:10 now
where the time goes in v1:
time: 304 us; the launch traced here: 300 us
  waiting for transfers between devices  107 us (35%)
  local copies, waits for them, and re-layouts  104 us (34%)
  matrix products  29.2 us (10%)
  blocking collectives  17.4 us (6%)
  starting transfers between devices  15.2 us (5%)
  between operations  13.9 us (5%)
  other arithmetic  13.5 us (4%)
    dynamic_update_slice x6, local copies, waits for them, and re-layouts, body(): lax.map(partial_attend, (all_queries, key_rows, value_rows, allowed))  53.2 us
    all_to_all x1, waiting for transfers between devices, body(): lax.all_to_all(outgoing, 'req', split_axis=0, concat_axis=0, tiled=True)  42.3 us
    ppermute x3, waiting for transfers between devices, body(): lax.ppermute(sent, 'req', [(i, i ^ lap) for i in range(size)])  41.5 us
    all_to_all x1, waiting for transfers between devices, body(): lax.all_to_all(part_out[None], 'seq', split_axis=2, concat_axis=0, tiled=...  12.6 us
    mul x2, local copies, waits for them, and re-layouts, body(): spread_out * factors[..., None]  11.1 us
    all_gather x1, blocking collectives, body(): fresh_rows = lax.all_gather(rotated, 'seq', axis=1, tiled=True)  10.8 us
    all_gather x1, waiting for transfers between devices, body(): all_queries = lax.all_gather(queries, 'seq', axis=1, tiled=True)  10.2 us
    dot_general x2, matrix products, partial_attend(): jnp.einsum('kgqn,nkd->qkgd', weights, value_heads, preferred_element_type...  9.64 us
  transfers between devices with their start and end apart: 6, of which 6 were waited for; matrix products, arithmetic and copies ran while one was open for 10% of the time, Pallas kernels for 0%

profile of v1, /device:TPU:10, one launch (start us, length us, event | category | flops | bytes accessed | tf_op | source)
XLA Modules:
  0.0 299.6 jit_solution(16553558773765664176)
XLA Ops:
  13.5 10.8 %all_gather.6 = bf16[2,256,512]{2,1,0:T(8,128)(2,1)S(1)} all-gather(bf16[2,32,512]{2,1,0:T(8,128)(2,1)S(1)} %convert_element_type.65), channel_id=1, replica_groups=mesh['seq'=8,'req'=4] {'seq'}, dimensions={1}, use_global_device_ids=true | all-gather | bytes 589824 | tf_op jit(solution)/shard_map/all_gather | solution.py:101
  27.0 10.2 %all-gather.2.cloned.1.call-done = bf16[2,256,1536]{2,0,1:T(2,128)(2,1)} async-done(((bf16[2,32,1536]{2,0,1:T(2,128)(2,1)}), bf16[2,256,1536]{2,0,1:T(2,128)(2,1)}) %all-gather.2.cloned.1.call-update) | async-done | bytes 1572880 | tf_op jit(solution)/shard_map/all_gather | solution.py:113
  37.3 4.9 %copy.75 = bf16[2,256,1536]{1,2,0:T(8,128)(2,1)} copy(bf16[2,256,1536]{2,0,1:T(2,128)(2,1)} %all-gather.2.cloned.1.call-done) | data formatting | bytes 3145728 | tf_op jit(solution)/shard_map/while | solution.py:127
  42.2 78.1 %while.12 = (s32[]{:T(128)}, f32[2,256,1536]{2,0,1:T(2,128)}, f32[2,256,24]{1,2,0:T(8,128)S(1)}, bf16[2,288,512]{1,2,0:T(8,128)(2,1)}, pred[2,256,288]{1,2,0:T(8...) while((s32[]{:T(128)}, f32[2,256,1536]{2,0,1:T(2,128)}, ...), condition=%wide.region_4.5_spmd, body=%wide.region_1.4_spmd.sunk | while | flops 472836096 | bytes 62791824 | solution.py:127
  49.8 4.8 %bitcast_divide_fusion.2 = f32[256,8,3,64]{0,3,2,1:T(8,128)S(1)} fusion(bf16[288,8,64,1]{0,2,3,1:T(8,128)(2,1)S(1)} %bitcast.184, f32[8,288,256,3]{2,1,3,0:T(8,128)} %copy-done.2, f32[8,3,256]{2,1,0:T(4,128)S(1)} %get-tuple-element.156, pred[256,288]{0,1:T(8,128)(4,1)S(1)} %dynamic-slice_bitcast_fusion.6, f32[256,8,3]{0,2,1:T(4,128)S(1)} %bitcast.186), kind=kOutput, calls=%fused_computation.9.clone.1 | convolution fusion | flops 233963520 | bytes 9068544 | tf_op jit(solution)/shard_map/while/body/eval_jaxpr/kgqn,nkd->qkgd/dot_general | solution.py:62
  55.8 25.4 %dynamic_update_slice.12 = f32[2,256,1536]{2,0,1:T(2,128)} dynamic-update-slice(f32[2,256,1536]{2,0,1:T(2,128)} %get-tuple-element.167, f32[1,256,1536]{2,0,1:T(1,128)S(1)} %copy.127, s32[]{:T(128)} %get-tuple-element.166, s32[]{:T(128)} %constant.49.clone.1..sunk, s32[]{:T(128)} %constant.49.clone.1..sunk) | dynamic-update-slice | bytes 3145732 | tf_op jit(solution)/shard_map/while/body/jit(dynamic_update_index_in_dim)/dynamic_update_slice | solution.py:127
  88.8 4.8 %bitcast_divide_fusion.2 = f32[256,8,3,64]{0,3,2,1:T(8,128)S(1)} fusion(bf16[288,8,64,1]{0,2,3,1:T(8,128)(2,1)S(1)} %bitcast.184, f32[8,288,256,3]{2,1,3,0:T(8,128)} %copy-done.2, f32[8,3,256]{2,1,0:T(4,128)S(1)} %get-tuple-element.156, pred[256,288]{0,1:T(8,128)(4,1)S(1)} %dynamic-slice_bitcast_fusion.6, f32[256,8,3]{0,2,1:T(4,128)S(1)} %bitcast.186), kind=kOutput, calls=%fused_computation.9.clone.1 | convolution fusion | flops 233963520 | bytes 9068544 | tf_op jit(solution)/shard_map/while/body/eval_jaxpr/kgqn,nkd->qkgd/dot_general | solution.py:62
  94.8 25.4 %dynamic_update_slice.12 = f32[2,256,1536]{2,0,1:T(2,128)} dynamic-update-slice(f32[2,256,1536]{2,0,1:T(2,128)} %get-tuple-element.167, f32[1,256,1536]{2,0,1:T(1,128)S(1)} %copy.127, s32[]{:T(128)} %get-tuple-element.166, s32[]{:T(128)} %constant.49.clone.1..sunk, s32[]{:T(128)} %constant.49.clone.1..sunk) | dynamic-update-slice | bytes 3145732 | tf_op jit(solution)/shard_map/while/body/jit(dynamic_update_index_in_dim)/dynamic_update_slice | solution.py:127
  120.8 6.6 %all_to_all.38 = f32[8,1,1536]{2,1,0:T(1,128)S(1)} all-to-all(f32[8,1,1536]{2,1,0:T(1,128)S(1)} %reshape.360), channel_id=1, replica_groups=mesh['seq'=8,'req'=4] {'seq'}, dimensions={0} | all-to-all | bytes 98304 | tf_op jit(solution)/shard_map/all_to_all | solution.py:130
  127.4 5.2 %all-to-all-start = ((f32[1,2,256,1536]{3,1,0,2:T(2,128)}), f32[1,2,256,1536]{3,1,0,2:T(2,128)S(1)}, u32[]{:S(2)}, u32[]{:S(2)}) async-start(f32[1,2,256,1536]{3,1,0,2:T(2,128)} %bitcast.187), calls=%async_computation | async-start | bytes 6291456 | tf_op jit(solution)/shard_map/all_to_all | solution.py:129
  141.9 4.9 %mul.189 = f32[8,2,32,24,64]{4,3,2,0,1:T(8,128)} broadcast(f32[8,2,32,24]{3,2,0,1:T(8,128)} %copy.80), dimensions={0,1,2,3} | broadcast | bytes 3194880 | tf_op jit(solution)/shard_map/mul | solution.py:136
  146.8 6.2 %mul.190 = f32[8,1,2,32,1536]{4,3,0,2,1:T(8,128)} reshape(f32[8,2,32,24,64]{4,3,2,0,1:T(8,128)} %mul.189) | data formatting | bytes 6291456 | tf_op jit(solution)/shard_map/mul | solution.py:136
  154.2 2.1 div.54
  156.4 12.6 %all-to-all-done = f32[1,2,256,1536]{3,1,0,2:T(2,128)S(1)} async-done(((f32[1,2,256,1536]{3,1,0,2:T(2,128)}), f32[1,2,256,1536]{3,1,0,2:T(2,128)S(1)}, u32[]{:S(2)}, u32[]{:S(2)}) %all-to-all-start) | async-done | bytes 3145760 | tf_op jit(solution)/shard_map/all_to_all | solution.py:129
  174.2 5.1 %all-to-all-start.2 = ((bf16[4,2,5,16,1536]{4,3,1,2,0:T(8,128)(2,1)}), bf16[4,2,5,16,1536]{4,3,1,2,0:T(8,128)(2,1)S(1)}, u32[]{:S(2)}, u32[]{:S(2)}) async-start(bf16[4,2,5,16,1536]{4,3,1,2,0:T(8,128)(2,1)} %copy.91), calls=%async_computation.2 | async-start | bytes 3932160 | tf_op jit(solution)/shard_map/all_to_all | solution.py:159
  179.4 42.3 %all-to-all-done.2 = bf16[4,2,5,16,1536]{4,3,1,2,0:T(8,128)(2,1)S(1)} async-done(((bf16[4,2,5,16,1536]{4,3,1,2,0:T(8,128)(2,1)}), bf16[4,2,5,16,1536]{4,3,1,2,0:T(8,128)(2,1)S(1)}, u32[]{:S(2)}, u32[]{:S(2)}) %all-to-all-start.2) | async-done | bytes 1966112 | tf_op jit(solution)/shard_map/all_to_all | solution.py:159
  221.7 7.7 %fusion.19 = f32[4,2,5,16,1024]{4,3,1,0,2:T(8,128)S(1)} fusion(bf16[5,1536,1024]{2,1,0:T(8,128)(2,1)} %param.24, bf16[4,2,5,16,1536]{4,3,1,2,0:T(8,128)(2,1)S(1)} %all-to-all-done.2), kind=kOutput, calls=%fused_computation.28 | convolution fusion | flops 2013265920 | bytes 20316160 | tf_op jit(solution)/shard_map/srecd,edf->srecf/dot_general | solution.py:157
  229.4 4.7 %fusion.14 = bf16[5,4,2,16,1536]{4,3,2,1,0:T(8,128)(2,1)S(1)} fusion(bf16[5,512,1536]{2,1,0:T(8,128)(2,1)} %param.25, f32[4,2,5,16,1024]{4,3,1,0,2:T(8,128)S(1)} %fusion.19), kind=kOutput, calls=%fused_computation.22 | convolution fusion | flops 1009582080 | bytes 12451840 | tf_op jit(solution)/shard_map/srecf,efd->srecd/dot_general | solution.py:164
  234.3 3.3 %collective-permute-start = (bf16[1,2,5,16,1536]{4,3,1,2,0:T(8,128)(2,1)S(1)}, bf16[1,2,5,16,1536]{4,3,1,2,0:T(8,128)(2,1)S(1)}, u32[]{:S(2)}, u32[]{:S(2)}) collective-permute-start(bf16[1,2,5,16,1536]{4,3,1,2,0:T(8,128)(2,1)S(1)} %get-tuple-element.98), channel_id=1, source_target_pairs={{0,1},{1,0},{2,3},{3,2},{4,5},{5,4},{6,7},{7,6},{8,9},{9,8},{10,11... | collective-permute-start | bytes 1474568 | tf_op jit(solution)/shard_map/ppermute | solution.py:172
  239.6 17.0 %collective-permute-done = bf16[1,2,5,16,1536]{4,3,1,2,0:T(8,128)(2,1)S(1)} collective-permute-done((bf16[1,2,5,16,1536]{4,3,1,2,0:T(8,128)(2,1)S(1)}, bf16[1,2,5,16,1536]{4,3,1,2,0:T(8,128)(2,1)S(1)}, u32[]{:S(2)}, u32[]{:S(2)}) %collective-permute-start) | collective-permute-done | bytes 491552 | tf_op jit(solution)/shard_map/ppermute | solution.py:172
  256.7 13.8 %collective-permute-done.1 = bf16[1,2,5,16,1536]{4,3,1,2,0:T(8,128)(2,1)S(1)} collective-permute-done((bf16[1,2,5,16,1536]{4,3,1,2,0:T(8,128)(2,1)S(1)}, bf16[1,2,5,16,1536]{4,3,1,2,0:T(8,128)(2,1)S(1)}, u32[]{:S(2)}, u32[]{:S(2)}) %collective-permute-start.1) | collective-permute-done | bytes 491552 | tf_op jit(solution)/shard_map/ppermute | solution.py:172
  270.4 10.7 %collective-permute-done.2 = bf16[1,2,5,16,1536]{4,3,1,0,2:T(8,128)(2,1)} collective-permute-done((bf16[1,2,5,16,1536]{4,3,1,0,2:T(8,128)(2,1)S(1)}, bf16[1,2,5,16,1536]{4,3,1,0,2:T(8,128)(2,1)}, u32[]{:S(2)}, u32[]{:S(2)}) %collective-permute-start.2) | collective-permute-done | bytes 491552 | tf_op jit(solution)/shard_map/ppermute | solution.py:172
  286.2 3.0 gather_fusion.1
  289.2 2.9 fusion.24
  (140 shorter events, 51.2 us)
Async XLA Ops:
  6.5 4.6 %copy-start = (bf16[2,32,1536]{2,1,0:T(8,128)(2,1)S(1)}, bf16[2,32,1536]{2,1,0:T(8,128)(2,1)}, u32[]{:S(2)}) copy-start(bf16[2,32,1536]{2,1,0:T(8,128)(2,1)} %param.19) | copy-start | bytes 589828
  6.5 30.7 %all-gather.2.cloned.1.call-start = ((), (), s32[]{:S(2)}) async-start(), calls=%async_computation.3 | async-start | bytes 1769472 | tf_op jit(solution)/shard_map/all_gather | solution.py:113
  10.9 1.6 copy-start.7
  12.0 1.0 slice-start
  12.1 1.1 copy-start.15
  12.3 12.2 %copy-start.14 = (s32[2,256]{1,0:T(2,128)S(1)}, s32[2,256]{1,0:T(2,128)}, u32[]{:S(2)}) copy-start(s32[2,256]{1,0:T(2,128)} %param.18) | copy-start | bytes 6148
  12.4 12.4 %copy-start.4 = (bf16[2,2,256,512]{3,2,1,0:T(8,128)(2,1)S(1)}, bf16[2,2,256,512]{3,2,1,0:T(8,128)(2,1)}, u32[]{:S(2)}) copy-start(bf16[2,2,256,512]{3,2,1,0:T(8,128)(2,1)} %param.16) | copy-start | bytes 3145732
  45.8 2.9 copy-start.2
  84.8 2.9 copy-start.2
  127.4 5.2 %copy-start.12 = (s32[2,32,8]{1,2,0:T(8,128)S(1)}, s32[2,32,8]{1,2,0:T(8,128)}, u32[]{:S(2)}) copy-start(s32[2,32,8]{1,2,0:T(8,128)} %param.22) | copy-start | bytes 6148
  127.4 41.5 %all-to-all-start = ((f32[1,2,256,1536]{3,1,0,2:T(2,128)}), f32[1,2,256,1536]{3,1,0,2:T(2,128)S(1)}, u32[]{:S(2)}, u32[]{:S(2)}) async-start(f32[1,2,256,1536]{3,1,0,2:T(2,128)} %bitcast.187), calls=%async_computation | async-start | bytes 6291456 | tf_op jit(solution)/shard_map/all_to_all | solution.py:129
  134.5 0.7 copy-start.9
  146.8 6.2 %copy-start.8 = (f32[2,32,24]{1,2,0:T(8,128)S(1)}, f32[2,32,24]{1,2,0:T(8,128)}, u32[]{:S(2)}) copy-start(f32[2,32,24]{1,2,0:T(8,128)} %get-tuple-element.93) | copy-start | bytes 18436
  169.0 1.9 copy-start.3
  170.8 1.0 copy-start.5
  170.8 1.1 copy-start.11
  174.2 47.5 %all-to-all-start.2 = ((bf16[4,2,5,16,1536]{4,3,1,2,0:T(8,128)(2,1)}), bf16[4,2,5,16,1536]{4,3,1,2,0:T(8,128)(2,1)S(1)}, u32[]{:S(2)}, u32[]{:S(2)}) async-start(bf16[4,2,5,16,1536]{4,3,1,2,0:T(8,128)(2,1)} %copy.91), calls=%async_computation.2 | async-start | bytes 3932160 | tf_op jit(solution)/shard_map/all_to_all | solution.py:159
  234.1 5.3 %copy-start.10 = (s32[2,256]{1,0:T(2,128)S(1)}, s32[2,256]{1,0:T(2,128)}, u32[]{:S(2)}) copy-start(s32[2,256]{1,0:T(2,128)} %copy-done.9) | copy-start | bytes 6148
  234.1 5.4 %copy-start.13 = (f32[2,32,8]{1,2,0:T(8,128)S(1)}, f32[2,32,8]{1,2,0:T(8,128)}, u32[]{:S(2)}) copy-start(f32[2,32,8]{1,2,0:T(8,128)} %param.23) | copy-start | bytes 6148
  234.3 22.4 %collective-permute-start = (bf16[1,2,5,16,1536]{4,3,1,2,0:T(8,128)(2,1)S(1)}, bf16[1,2,5,16,1536]{4,3,1,2,0:T(8,128)(2,1)S(1)}, u32[]{:S(2)}, u32[]{:S(2)}) collective-permute-start(bf16[1,2,5,16,1536]{4,3,1,2,0:T(8,128)(2,1)S(1)} %get-tuple-element.98), channel_id=1, source_target_pairs={{0,1},{1,0},{2,3},{3,2},{4,5},{5,4},{6,7},{7,6},{8,9},{9,8},{10,11... | collective-permute-start | bytes 1474568 | tf_op jit(solution)/shard_map/ppermute | solution.py:172
  237.6 32.8 %collective-permute-start.1 = (bf16[1,2,5,16,1536]{4,3,1,2,0:T(8,128)(2,1)S(1)}, bf16[1,2,5,16,1536]{4,3,1,2,0:T(8,128)(2,1)S(1)}, u32[]{:S(2)}, u32[]{:S(2)}) collective-permute-start(bf16[1,2,5,16,1536]{4,3,1,2,0:T(8,128)(2,1)S(1)} %get-tuple-element.100), channel_id=1, source_target_pairs={{0,2},{1,3},{2,0},{3,1},{4,6},{5,7},{6,4},{7,5},{8,10},{9,11},{10,... | collective-permute-start | bytes 1474568 | tf_op jit(solution)/shard_map/ppermute | solution.py:172
  237.7 43.4 %collective-permute-start.2 = (bf16[1,2,5,16,1536]{4,3,1,0,2:T(8,128)(2,1)S(1)}, bf16[1,2,5,16,1536]{4,3,1,0,2:T(8,128)(2,1)}, u32[]{:S(2)}, u32[]{:S(2)}) collective-permute-start(bf16[1,2,5,16,1536]{4,3,1,0,2:T(8,128)(2,1)S(1)} %get-tuple-element.99), channel_id=1, source_target_pairs={{0,3},{1,2},{2,1},{3,0},{4,7},{5,6},{6,5},{7,4},{8,11},{9,10},{10,... | collective-permute-start | bytes 1474568 | tf_op jit(solution)/shard_map/ppermute | solution.py:172
  270.4 10.7 %copy-start.6 = (bf16[1,2,5,16,1536]{4,3,1,2,0:T(8,128)(2,1)}, bf16[1,2,5,16,1536]{4,3,1,2,0:T(8,128)(2,1)S(1)}, u32[]{:S(2)}) copy-start(bf16[1,2,5,16,1536]{4,3,1,2,0:T(8,128)(2,1)S(1)} %collective-permute-done.1) | copy-start | bytes 1474564
  286.2 6.6 %copy-start.1 = (bf16[2,32,1536]{2,1,0:T(8,128)(2,1)S(1)}, bf16[2,32,1536]{2,1,0:T(8,128)(2,1)}, u32[]{:S(2)}) copy-start(bf16[2,32,1536]{2,1,0:T(8,128)(2,1)} %param.19) | copy-start | bytes 589828
Sparse Core Ops, SparseCore 0:
  9.2 27.9 all-gather.1
